TPU v7x, 32 devices: a whole 2x2x4 slice. The times are simulated.
32 devices in a mesh: sub: 8 (over z, y), col: 4 (over x, core).
Axes of the slice: x: 2, y: 2, z: 4, core: 2. Of those that a mesh axis runs over, the one named last changes fastest.
Arguments:
- rhs: bfloat16 [32, 1024, 128], P(('sub', 'col')), may hold values from -64 to 64
- schur: bfloat16 [32, 1024, 1024], P(('sub', 'col')), may hold values from -1 to 3
- local_inverse: bfloat16 [32, 1024, 1024], P(('sub', 'col')), may hold values from -1 to 2
- basis: bfloat16 [32, 8, 1024], P(('sub', 'col')), may hold values from -0.75 to 0.75
- coarse_inverse: bfloat16 [256, 256], P('sub', 'col'), may hold values from -1 to 2
- primal_index: int32 [32, 8], P(('sub', 'col')), may hold values from 0 to 255, as said below
- neighbour_dof: int32 [32, 1024], P(('sub', 'col')), may hold values from 0 to 1023, as said below
Outputs:
- solution: bfloat16 [32, 1024, 128], P(('sub', 'col'))
Inputs may be any that keep to these rules, and one draw needn't show every extreme that they name: `neighbour_dof`: each subdomain's unknowns in one shared block name places in the neighbour's facing block (for [0, 256) the neighbour's [256, 512), and so on), and the neighbour's entry names the place back. `primal_index`: every coarse unknown is named exactly once over all subdomains.
All inputs are finite; a program needn't handle non-finite values.
Results may differ from a plain program's by a relative error of at most 0.004.
The roundings to bfloat16 on the way count: a program that leaves them out, or rounds other values in their place, can miss the bound.
Values may be sent and summed in bfloat16 or wider, within the bound.
A program may use at most 64 MiB of HBM per device.

v0:
```python
import functools
import math

import jax
import jax.numpy as jnp
from jax import lax
from jax.experimental import pallas as pl
from jax.experimental.pallas import tpu as pltpu
from jax.sharding import PartitionSpec as P

MESH = pl.DeviceIdType.MESH
F32 = jnp.float32
BF16 = jnp.bfloat16
UNROLL = True


def kernel(
    subs, cols,
    rhs_hbm, schur_hbm, inverse_hbm, basis_hbm, coarse_hbm, index_hbm, links_hbm,
    first_ref, alpha_ref,
    basis_ref, coarse_ref, index_ref, links_ref,
    rhs_ref, schur_ref, inverse_ref, picks, halo_rhs, halo_z, weighted, z_ref, z_half, p_half,
    image_ref, indices, chosen, arrived, columns, rows_ref, loads, sums,
    local_sem, halo_send, halo_recv, z_send, z_recv, all_send, all_recv,
):
    count = subs * cols
    row = lax.axis_index("sub")
    column = lax.axis_index("col")
    me = row * cols + column
    size = rhs_ref.shape[0]
    face = size // 4
    primals = index_ref.shape[1]
    height, width = coarse_ref.shape
    group = math.gcd(count, 32)

    def place(target):
        return (target // cols, target % cols)

    half_way = (row * 2) // subs

    def each_other(act):
        def body(step, carry):
            q = step // cols
            target_row = (1 - half_way) * (subs - 1 - q) + half_way * q
            target = target_row * cols + (column + step) % cols

            @pl.when(target != me)
            def _():
                act(target)

            return carry

        lax.fori_loop(0, count, body, 0, unroll=UNROLL and count <= 64)

    barrier = pltpu.get_barrier_semaphore()

    each_other(
        lambda target: pl.semaphore_signal(
            barrier, inc=1, device_id=place(target), device_id_type=MESH
        )
    )

    small_loads = [
        pltpu.make_async_copy(source, target, local_sem.at[4 + number])
        for number, (source, target) in enumerate(
            ((links_hbm, links_ref), (index_hbm, index_ref), (basis_hbm, basis_ref), (coarse_hbm, coarse_ref))
        )
    ]
    for load in small_loads:
        load.start()
    load_rhs = pltpu.make_async_copy(rhs_hbm.at[0], rhs_ref, local_sem.at[0])
    load_inverse = pltpu.make_async_copy(inverse_hbm.at[0], inverse_ref, local_sem.at[1])
    load_schur = pltpu.make_async_copy(schur_hbm.at[0], schur_ref, local_sem.at[2])
    load_rhs.start()
    load_inverse.start()
    load_schur.start()
    for load in small_loads:
        load.wait()

    lanes = indices.shape[2]
    indices[me] = jnp.zeros((1, lanes), F32)
    indices[me, :, pl.ds(0, primals)] = index_ref[...].astype(F32)

    offsets = (face, 0, 3 * face, 2 * face)
    for f in range(4):
        places = links_ref[:, f * face : (f + 1) * face] - offsets[f]
        hit = lax.broadcasted_iota(jnp.int32, (face, face), 0) == places
        picks[f] = jnp.where(hit, 1.0, 0.0).astype(F32).T.astype(BF16)

    pl.semaphore_wait(barrier, count - 1)

    swap = row % 2

    def halo_copies(source, target, send, recv):
        copies = []
        for g in (swap, 1 - swap, 2, 3):
            if isinstance(g, int):
                facing = 5 - g
                partner = (row, (column + cols + 2 * g - 5) % cols)
            else:
                facing = 1 - g
                partner = ((row + subs + 2 * g - 1) % subs, column)
            copies.append(
                pltpu.make_async_remote_copy(
                    src_ref=source(g),
                    dst_ref=target.at[facing],
                    send_sem=send.at[g],
                    recv_sem=recv.at[facing],
                    device_id=partner,
                    device_id_type=MESH,
                )
            )
        return copies

    def wait_face(target, recv, f):
        pltpu.make_async_copy(target.at[f], target.at[f], recv.at[f]).wait()

    def broadcast(slots, number):
        each_other(
            lambda target: pltpu.make_async_remote_copy(
                src_ref=slots.at[me],
                dst_ref=slots.at[me],
                send_sem=all_send.at[number],
                recv_sem=all_recv.at[number],
                device_id=place(target),
                device_id_type=MESH,
            ).start()
        )

    def wait_all(slots, sems, number):
        part = slots.at[pl.ds(0, count - 1)]
        pltpu.make_async_copy(part, part, sems.at[number]).wait()

    rhs_copies = halo_copies(
        lambda g: rhs_hbm.at[0, pl.ds(g * face, face)], halo_rhs, halo_send, halo_recv
    )
    broadcast(indices, 0)
    for copy in rhs_copies:
        copy.start()

    basis = basis_ref[0]
    basis_t = basis.astype(F32).T.astype(BF16)
    load_rhs.wait()

    wait_all(indices, all_recv, 0)

    def spread(g, extent):
        values = indices[pl.ds(g * group, group)]
        values = jnp.broadcast_to(values, (group, primals, lanes))
        diagonal = lax.broadcasted_iota(jnp.int32, values.shape, 1) == lax.broadcasted_iota(
            jnp.int32, values.shape, 2
        )
        named = jnp.sum(jnp.where(diagonal, values, 0.0), axis=2, keepdims=True)
        named = named.astype(jnp.int32)
        return jnp.broadcast_to(named, (group, primals, extent))

    def choose(g, carry):
        named = spread(g, height) - row * height
        hit = lax.broadcasted_iota(jnp.int32, named.shape, 2) == named
        hit = jnp.where(hit, 1.0, 0.0).astype(F32).reshape(group * primals, height).astype(BF16)
        picked = jnp.dot(hit, coarse_ref[...], preferred_element_type=F32)
        chosen[pl.ds(g * group, group)] = picked.reshape(group, primals, width).astype(BF16)
        return carry

    lax.fori_loop(0, count // group, choose, 0)
    arrived[me] = chosen[me]

    each_other(
        lambda target: pltpu.make_async_remote_copy(
            src_ref=chosen.at[target],
            dst_ref=arrived.at[me],
            send_sem=all_send.at[2],
            recv_sem=all_recv.at[2],
            device_id=place(target),
            device_id_type=MESH,
        ).start()
    )

    load = jnp.zeros((primals, rhs_ref.shape[1]), F32)
    for f in (2, 3, 0, 1):
        block = pl.ds(f * face, face)
        wait_face(halo_rhs, halo_recv, f)
        got = jnp.dot(picks[f], halo_rhs[f], preferred_element_type=F32)
        residual = rhs_ref[block, :].astype(F32) + got
        first_ref[block, :] = residual
        part = (residual * 0.5).astype(BF16)
        weighted[block, :] = part
        load += jnp.dot(basis[:, f * face : (f + 1) * face], part, preferred_element_type=F32)
    loads[me] = load.astype(BF16)
    broadcast(loads, 1)

    load_inverse.wait()
    for f in range(4):
        block = pl.ds(f * face, face)
        z_ref[block, :] = jnp.dot(inverse_ref[block, :], weighted[...], preferred_element_type=F32)

    wait_all(arrived, all_recv, 2)
    for j in range(cols):
        def add(i, total):
            return total + arrived[i * cols + j].astype(F32)

        rows_ref[j] = lax.fori_loop(0, subs, add, jnp.zeros((primals, width), F32), unroll=subs <= 8)

    def arrange(g, carry):
        total = jnp.zeros((primals, group * primals), F32)
        for j in range(cols):
            named = spread(g, width) - j * width
            hit = lax.broadcasted_iota(jnp.int32, named.shape, 2) == named
            hit = jnp.where(hit, 1.0, 0.0).astype(F32).reshape(group * primals, width).astype(BF16)
            total += lax.dot_general(
                rows_ref[j].astype(BF16), hit, (((1,), (1,)), ((), ())), preferred_element_type=F32
            )
        columns[g] = total
        return carry

    lax.fori_loop(0, count // group, arrange, 0)

    wait_all(loads, all_recv, 1)

    def solve(g, total):
        part = loads[pl.ds(g * group, group)].astype(F32).reshape(group * primals, loads.shape[2])
        return total + jnp.dot(columns[g].astype(BF16), part.astype(BF16), preferred_element_type=F32)

    taken = lax.fori_loop(
        0, count // group, solve, jnp.zeros((primals, loads.shape[2]), F32)
    ).astype(BF16)

    z_copies = halo_copies(lambda g: z_half.at[pl.ds(g * face, face)], halo_z, z_send, z_recv)
    for f in range(4):
        block = pl.ds(f * face, face)
        correction = jnp.dot(
            basis_t[f * face : (f + 1) * face, :], taken, preferred_element_type=F32
        )
        z_value = (z_ref[block, :] + correction) * 0.5
        z_ref[block, :] = z_value
        z_half[block, :] = z_value.astype(BF16)
        if f == 1:
            z_copies[0].start()
            z_copies[1].start()
        if f > 1:
            z_copies[f].start()
    sums[me, pl.ds(0, 1), :] = jnp.sum(first_ref[...] * z_ref[...], axis=0, keepdims=True)
    load_schur.wait()
    for pair in ((2, 3), (0, 1)):
        for f in pair:
            block = pl.ds(f * face, face)
            wait_face(halo_z, z_recv, f)
            first = z_ref[block, :] + jnp.dot(picks[f], halo_z[f], preferred_element_type=F32)
            first_ref[block, :] = first
            p_half[block, :] = first.astype(BF16)
        both = pl.ds(pair[0] * face, 2 * face)
        if pair[0] == 2:
            for f in range(4):
                block = pl.ds(f * face, face)
                image_ref[block, :] = jnp.dot(
                    schur_ref[block, both], p_half[both, :], preferred_element_type=F32
                )
    total = jnp.zeros((1, first_ref.shape[1]), F32)
    for f in range(4):
        block = pl.ds(f * face, face)
        image = image_ref[block, :] + jnp.dot(
            schur_ref[block, both], p_half[both, :], preferred_element_type=F32
        )
        total += jnp.sum(first_ref[block, :] * image, axis=0, keepdims=True)
    sums[me, pl.ds(1, 1), :] = total
    broadcast(sums, 3)
    for copy in rhs_copies + z_copies:
        copy.wait_send()
    wait_all(indices, all_send, 0)
    wait_all(loads, all_send, 1)
    wait_all(arrived, all_send, 2)
    wait_all(sums, all_recv, 3)
    whole = jnp.sum(sums[...], axis=0)
    alpha_ref[...] = whole[0:1, :] / whole[1:2, :]
    wait_all(sums, all_send, 3)


def solution(mesh):
    subs, cols = mesh.shape["sub"], mesh.shape["col"]
    count = subs * cols

    def step(rhs, schur, local_inverse, basis, coarse_inverse, primal_index, neighbour_dof):
        size, cases = rhs.shape[1:]
        face = size // 4
        primals = primal_index.shape[1]
        height, width = coarse_inverse.shape
        lanes = 128 * pl.cdiv(primals, 128)
        anywhere = pl.BlockSpec(memory_space=pltpu.HBM)
        near = pl.BlockSpec(memory_space=pltpu.VMEM)
        fixed = 4 * size * size + 8 * face * face + 22 * size * cases
        slots = count * (4 * 8 * lanes + 8 * primals * width + 4 * primals * cases + 4 * 8 * cases)
        blocks = 4 * primals * (count * primals + cols * width)
        group = math.gcd(count, 32)
        limit = min(fixed + slots + blocks + 4 * 1024 * 1024, 63 * 1024 * 1024)
        first, alpha = pl.pallas_call(
            functools.partial(kernel, subs, cols),
            out_shape=(
                jax.ShapeDtypeStruct((size, cases), F32),
                jax.ShapeDtypeStruct((1, cases), F32),
            ),
            in_specs=[anywhere] * 7,
            out_specs=(near, near),
            scratch_shapes=[
                pltpu.VMEM(basis.shape, BF16),
                pltpu.VMEM(coarse_inverse.shape, BF16),
                pltpu.VMEM(primal_index.shape, jnp.int32),
                pltpu.VMEM(neighbour_dof.shape, jnp.int32),
                pltpu.VMEM((size, cases), BF16),
                pltpu.VMEM((size, size), BF16),
                pltpu.VMEM((size, size), BF16),
                pltpu.VMEM((4, face, face), BF16),
                pltpu.VMEM((4, face, cases), BF16),
                pltpu.VMEM((4, face, cases), BF16),
                pltpu.VMEM((size, cases), BF16),
                pltpu.VMEM((size, cases), F32),
                pltpu.VMEM((size, cases), BF16),
                pltpu.VMEM((size, cases), BF16),
                pltpu.VMEM((size, cases), F32),
                pltpu.VMEM((count, 1, lanes), F32),
                pltpu.VMEM((count, primals, width), BF16),
                pltpu.VMEM((count, primals, width), BF16),
                pltpu.VMEM((count // group, primals, group * primals), F32),
                pltpu.VMEM((cols, primals, width), F32),
                pltpu.VMEM((count, primals, cases), BF16),
                pltpu.VMEM((count, 2, cases), F32),
                pltpu.SemaphoreType.DMA((8,)),
                pltpu.SemaphoreType.DMA((4,)),
                pltpu.SemaphoreType.DMA((4,)),
                pltpu.SemaphoreType.DMA((4,)),
                pltpu.SemaphoreType.DMA((4,)),
                pltpu.SemaphoreType.DMA((4,)),
                pltpu.SemaphoreType.DMA((4,)),
            ],
            compiler_params=pltpu.CompilerParams(
                collective_id=0, has_side_effects=True, vmem_limit_bytes=limit
            ),
        )(*(pltpu.with_memory_space_constraint(x, pltpu.HBM) for x in (rhs, schur, local_inverse, basis, coarse_inverse, primal_index, neighbour_dof)))
        return (alpha * first).astype(BF16)[None]

    return jax.shard_map(
        step,
        mesh=mesh,
        in_specs=(
            P(("sub", "col"), None, None),
            P(("sub", "col"), None, None),
            P(("sub", "col"), None, None),
            P(("sub", "col"), None, None),
            P("sub", "col"),
            P(("sub", "col"), None),
            P(("sub", "col"), None),
        ),
        out_specs=P(("sub", "col"), None, None),
        check_vma=False,
    )
```

profile of v0, /device:TPU:0, one launch (start us, length us, event | category | flops | bytes accessed | tf_op | source)
XLA Modules:
  0.0 28.8 jit_solution(9522762641817895220)
XLA Ops:
  0.0 28.1 %shard_map.73 = (f32[1024,128]{1,0:T(8,128)S(1)}, f32[1,128]{1,0:T(1,128)S(1)}) custom-call(bf16[1,1024,128]{2,1,0:T(8,128)(2,1)} %rhs_hbm.1, bf16[1,1024,1024]{2,1,0:T(8,128)(2,1)} %schur_hbm.1, bf16[1,1024,1024]{2,1,0:T(8,128)(2,1)} %inverse_hbm.1, bf16[1,8,1024]{2,1,0:T(8,128)(2,1)} %basis_hbm.1, bf16[32,64]{1,0:T(8,128)(2,1)} %coarse_hbm.1, ...), custom_call_target="tpu_custom_call" | custom-call | tf_op jit(solution)/shard_map/pallas_call | solution.py:295
  28.1 0.7 %fusion = bf16[1,1024,128]{2,1,0:T(8,128)(2,1)} fusion(f32[1024,128]{1,0:T(8,128)S(1)} %get-tuple-element.8, f32[128]{0:T(128)S(1)} %bitcast.3), kind=kLoop, calls=%fused_computation.1 | loop fusion | flops 262144 | bytes 786944 | tf_op jit(solution)/shard_map/broadcast_in_dim | solution.py:338
where the time goes:
time: 29 us; the launch traced here: 28.8 us
  Pallas kernels  28.1 us (97%)
  other arithmetic  0.73 us (3%)
    pallas_call x1, Pallas kernels, step(): pl.pallas_call(functools.partial(kernel, subs, cols), out_shape=(jax.Shap...  28.1 us
    broadcast_in_dim x1, other arithmetic, step(): return (alpha * first).astype(BF16)[None]  0.73 us

commit v1 on v0

v1 whole, which is shorter than its diff:
```python
import functools
import math

import jax
import jax.numpy as jnp
from jax import lax
from jax.experimental import pallas as pl
from jax.experimental.pallas import tpu as pltpu
from jax.sharding import PartitionSpec as P

MESH = pl.DeviceIdType.MESH
F32 = jnp.float32
BF16 = jnp.bfloat16


def kernel(
    subs, cols,
    rhs_hbm, schur_hbm, inverse_hbm, basis_hbm, coarse_hbm, index_hbm, links_hbm,
    first_ref, alpha_ref,
    basis_ref, index_ref, links_ref, rhs_ref, schur_ref, inverse_ref,
    picks, halo_rhs, halo_z, halo_basis, lift, given, z_ref, z_half, p_half, image_ref,
    indices, slab, picked, chosen, arrived, columns, loads, sums,
    local_sem, halo_send, halo_recv, z_send, z_recv, basis_send, basis_recv, all_send, all_recv,
    face_ack, all_ack,
):
    count = subs * cols
    row = lax.axis_index("sub")
    column = lax.axis_index("col")
    me = row * cols + column
    size = rhs_ref.shape[0]
    face = size // 4
    primals = index_ref.shape[1]
    height, width = coarse_hbm.shape
    cases = rhs_ref.shape[1]
    blocks = 5 * primals
    group = math.gcd(count, 32)
    straight = count <= 64

    def place(target):
        return (target // cols, target % cols)

    def span(f):
        return pl.ds(pl.multiple_of(f * face, face), face)

    half_way = (row * 2) // subs

    def each_other(act):
        def body(step, carry):
            q = step // cols
            high, low = subs - 1 - q, q
            high = high - (row - high + subs) // subs
            low = low + (low - row + subs) // subs
            target_row = (1 - half_way) * high + half_way * low
            act((target_row, (column + step) % cols))
            return carry

        lax.fori_loop(0, (subs - 1) * cols, body, 0, unroll=straight)
        for step in range(1, cols):
            act((row, (column + step) % cols))

    def loop(start, stop, act):
        def body(target, carry):
            act(target)
            return carry

        lax.fori_loop(start, stop, body, 0)

    barrier = pltpu.get_barrier_semaphore()
    loop(
        me + 1, count,
        lambda target: pl.semaphore_signal(
            barrier, inc=1, device_id=place(target), device_id_type=MESH
        ),
    )

    small_loads = [
        pltpu.make_async_copy(source, target, local_sem.at[4 + number])
        for number, (source, target) in enumerate(
            ((links_hbm, links_ref), (index_hbm, index_ref), (basis_hbm, basis_ref),
             (coarse_hbm, slab.at[pl.ds(row * height, height)]))
        )
    ]
    for load in small_loads:
        load.start()
    load_rhs = pltpu.make_async_copy(rhs_hbm.at[0], rhs_ref, local_sem.at[0])
    load_inverse = pltpu.make_async_copy(inverse_hbm.at[0], inverse_ref, local_sem.at[1])
    load_schur = pltpu.make_async_copy(schur_hbm.at[0], schur_ref, local_sem.at[2])
    load_rhs.start()
    load_inverse.start()
    load_schur.start()

    def facing(g):
        return 1 - g if g < 2 else 5 - g

    def partner(g):
        if g < 2:
            return ((row + subs + 2 * g - 1) % subs, column)
        return (row, (column + cols + 2 * g - 5) % cols)

    def exchange(source, target, send, recv, g):
        return pltpu.make_async_remote_copy(
            src_ref=source, dst_ref=target.at[facing(g)], send_sem=send.at[g], recv_sem=recv.at[facing(g)],
            device_id=partner(g), device_id_type=MESH,
        )

    rhs_copies = [
        exchange(rhs_hbm.at[0, pl.ds(g * face, face)], halo_rhs, halo_send, halo_recv, g) for g in range(4)
    ]
    basis_copies = [
        exchange(basis_hbm.at[0, :, pl.ds(g * face, face)], halo_basis, basis_send, basis_recv, g)
        for g in range(4)
    ]
    z_copies = [
        exchange(z_half.at[pl.ds(g * face, face)], halo_z, z_send, z_recv, g) for g in range(4)
    ]

    def row_z_copy(g):
        return pltpu.make_async_remote_copy(
            src_ref=z_half.at[span(g)], dst_ref=halo_z.at[1 - g], send_sem=z_send.at[g], recv_sem=z_recv.at[1 - g],
            device_id=((row + subs + 2 * g - 1) % subs, column), device_id_type=MESH,
        )

    lower = (row > 0, row == subs - 1, column > 0, column == cols - 1)
    higher = (row == 0, row < subs - 1, column == 0, column < cols - 1)

    @pl.when(me > 0)
    def _():
        pl.semaphore_wait(barrier, me)

    for g in (1, 0, 2, 3):
        @pl.when(lower[g])
        def _(g=g):
            pl.semaphore_signal(
                face_ack.at[facing(g)], inc=1, device_id=partner(g), device_id_type=MESH
            )
            rhs_copies[g].start()
            basis_copies[g].start()

    loop(
        0, me,
        lambda target: pl.semaphore_signal(
            all_ack.at[0], inc=1, device_id=place(target), device_id_type=MESH
        ),
    )

    def send_coarse(target):
        pltpu.make_async_remote_copy(
            src_ref=coarse_hbm,
            dst_ref=slab.at[pl.ds(row * height, height)],
            send_sem=all_send.at[4],
            recv_sem=all_recv.at[4],
            device_id=(target, column),
            device_id_type=MESH,
        ).start()

    def send_slot(slots, number):
        return lambda target: pltpu.make_async_remote_copy(
            src_ref=slots.at[me],
            dst_ref=slots.at[me],
            send_sem=all_send.at[number],
            recv_sem=all_recv.at[number],
            device_id=target,
            device_id_type=MESH,
        ).start()

    loop(0, row, send_coarse)
    for load in small_loads:
        load.wait()
    lanes = indices.shape[2]
    indices[me] = jnp.zeros((1, lanes), F32)
    indices[me, :, pl.ds(0, primals)] = index_ref[...].astype(F32)
    loop(0, me, lambda target: send_slot(indices, 0)(place(target)))

    offsets = (face, 0, 3 * face, 2 * face)
    for f in range(4):
        places = links_ref[:, f * face : (f + 1) * face] - offsets[f]
        hit = lax.broadcasted_iota(jnp.int32, (face, face), 0) == places
        picks[f] = jnp.where(hit, 1.0, 0.0).astype(F32).T.astype(BF16)

    for g in (3, 2, 1, 0):
        @pl.when(higher[g])
        def _(g=g):
            pl.semaphore_wait(face_ack.at[g], 1)
            rhs_copies[g].start()
            basis_copies[g].start()

    @pl.when(me < count - 1)
    def _():
        pl.semaphore_wait(all_ack.at[0], count - 1 - me)

    loop(row + 1, subs, send_coarse)
    loop(me + 1, count, lambda target: send_slot(indices, 0)(place(target)))

    def wait_face(target, recv, f):
        pltpu.make_async_copy(target.at[f], target.at[f], recv.at[f]).wait()

    def wait_part(part, sems, number):
        pltpu.make_async_copy(part, part, sems.at[number]).wait()

    others = pl.ds(0, count - 1)

    last = (row + 1) // subs
    load_rhs.wait()
    load = jnp.zeros((primals, cases), F32)
    load_inverse.wait()
    for number, f in enumerate((2, 3, 1 - last, last)):
        block = span(f)
        wait_face(halo_rhs, halo_recv, f)
        got = jnp.dot(picks[f], halo_rhs[f], preferred_element_type=F32)
        residual = rhs_ref[block, :].astype(F32) + got
        first_ref[block, :] = residual
        part = (residual * 0.5).astype(BF16)
        load += jnp.dot(basis_ref[0, :, block], part, preferred_element_type=F32)
        if number == 0:
            for h in range(4):
                rows = span(h)
                z_ref[rows, :] = jnp.dot(inverse_ref[rows, block], part, preferred_element_type=F32)
        elif number < 3:
            for h in range(4):
                rows = span(h)
                z_ref[rows, :] += jnp.dot(inverse_ref[rows, block], part, preferred_element_type=F32)
        else:
            for turn, h in enumerate((last, 1 - last, 2, 3)):
                rows = span(h)
                value = z_ref[rows, :] + jnp.dot(inverse_ref[rows, block], part, preferred_element_type=F32)
                value = value * 0.5
                z_ref[rows, :] = value
                z_half[rows, :] = value.astype(BF16)
                (row_z_copy(h) if turn < 2 else z_copies[h]).start()
                if turn == 0:
                    loads[me] = load.astype(BF16)
                    each_other(send_slot(loads, 1))
    begun = jnp.sum(first_ref[...] * z_ref[...], axis=0, keepdims=True)

    def spread(start, extent, number):
        values = indices[pl.ds(start, number)]
        values = jnp.broadcast_to(values, (number, primals, lanes))
        diagonal = lax.broadcasted_iota(jnp.int32, values.shape, 1) == lax.broadcasted_iota(
            jnp.int32, values.shape, 2
        )
        named = jnp.sum(jnp.where(diagonal, values, 0.0), axis=2, keepdims=True)
        named = named.astype(jnp.int32)
        return jnp.broadcast_to(named, (number, primals, extent))

    wait_part(indices.at[others], all_recv, 0)
    total_rows = subs * height
    chunk = math.gcd(total_rows, 256)
    own = spread(row * cols, chunk, cols)
    up = spread((row + subs - 1) % subs * cols, chunk, cols)
    down = spread((row + 1) % subs * cols, chunk, cols)
    named = jnp.concatenate(
        [
            source[k : k + 1]
            for j in range(cols)
            for source, k in ((own, j), (up, j), (down, j), (own, (j + cols - 1) % cols), (own, (j + 1) % cols))
        ],
        axis=0,
    )
    wait_part(slab.at[pl.ds(0, (subs - 1) * height)], all_recv, 4)

    def choose(k, carry):
        hit = lax.broadcasted_iota(jnp.int32, named.shape, 2) == named - k * chunk
        hit = jnp.where(hit, 1.0, 0.0).astype(F32).reshape(cols * blocks, chunk).astype(BF16)
        part = slab[pl.ds(pl.multiple_of(k * chunk, chunk), chunk), :]
        picked[...] += jnp.dot(hit, part, preferred_element_type=F32)
        return carry

    picked[...] = jnp.zeros_like(picked)
    lax.fori_loop(0, total_rows // chunk, choose, 0)
    chosen[...] = picked[...].reshape(cols, blocks, width).astype(BF16)
    arrived[column] = chosen[column]
    for step in range(1, cols):
        target = (column + step) % cols
        pltpu.make_async_remote_copy(
            src_ref=chosen.at[target],
            dst_ref=arrived.at[column],
            send_sem=all_send.at[3],
            recv_sem=all_recv.at[3],
            device_id=(row, target),
            device_id_type=MESH,
        ).start()

    for f in range(4):
        wait_face(halo_basis, basis_recv, f)
        mine = basis_ref[0, :, f * face : (f + 1) * face].astype(F32) * 0.5
        theirs = halo_basis[f].astype(F32) * 0.5
        both = jnp.concatenate([jnp.zeros_like(theirs), theirs], axis=0).astype(BF16)
        turned = lax.dot_general(picks[f], both, (((1,), (1,)), ((), ())), preferred_element_type=F32)
        kept = jnp.concatenate([mine, jnp.zeros_like(mine)], axis=0).T
        lift[f] = (turned + kept).astype(BF16)

    wait_part(arrived.at[pl.ds(0, cols - 1)], all_recv, 3)

    def arrange(g, carry):
        total = jnp.zeros((blocks, group * primals), F32)
        for j in range(cols):
            named = spread(g * group, width, group) - j * width
            hit = lax.broadcasted_iota(jnp.int32, named.shape, 2) == named
            hit = jnp.where(hit, 1.0, 0.0).astype(F32).reshape(group * primals, width).astype(BF16)
            total += lax.dot_general(
                arrived[j], hit, (((1,), (1,)), ((), ())), preferred_element_type=F32
            )
        columns[g] = total.astype(BF16)
        return carry

    lax.fori_loop(0, count // group, arrange, 0)

    wait_part(loads.at[others], all_recv, 1)

    def solve(g, total):
        part = loads[pl.ds(g * group, group)].astype(F32).reshape(group * primals, cases)
        return total + jnp.dot(columns[g], part.astype(BF16), preferred_element_type=F32)

    taken = lax.fori_loop(0, count // group, solve, jnp.zeros((blocks, cases), F32))
    taken = taken.astype(BF16).astype(F32)
    for f in range(4):
        given[f] = jnp.concatenate(
            [taken[:primals], taken[(f + 1) * primals : (f + 2) * primals]], axis=0
        ).astype(BF16)
    ended = jnp.sum(load * taken[:primals], axis=0, keepdims=True)
    sums[me, pl.ds(0, 1), :] = begun + ended

    load_schur.wait()
    for number, f in enumerate((2, 3, 1 - last, last)):
        block = span(f)
        first = z_ref[block, :] + jnp.dot(lift[f], given[f], preferred_element_type=F32)
        wait_face(halo_z, z_recv, f)
        first = first + jnp.dot(picks[f], halo_z[f], preferred_element_type=F32)
        first_ref[block, :] = first
        part = first.astype(BF16)
        if number == 0:
            for h in range(4):
                rows = span(h)
                image_ref[rows, :] = jnp.dot(schur_ref[rows, block], part, preferred_element_type=F32)
        elif number < 3:
            for h in range(4):
                rows = span(h)
                image_ref[rows, :] += jnp.dot(schur_ref[rows, block], part, preferred_element_type=F32)
        else:
            total = jnp.zeros((1, cases), F32)
            for h in range(4):
                rows = span(h)
                image = image_ref[rows, :] + jnp.dot(
                    schur_ref[rows, block], part, preferred_element_type=F32
                )
                total += jnp.sum(first_ref[rows, :] * image, axis=0, keepdims=True)
    sums[me, pl.ds(1, 1), :] = total
    each_other(send_slot(sums, 2))
    for copy in rhs_copies + basis_copies + z_copies:
        copy.wait_send()
    wait_part(indices.at[others], all_send, 0)
    wait_part(loads.at[others], all_send, 1)
    wait_part(arrived.at[pl.ds(0, cols - 1)], all_send, 3)
    wait_part(slab.at[pl.ds(0, (subs - 1) * height)], all_send, 4)
    wait_part(sums.at[others], all_recv, 2)
    whole = jnp.sum(sums[...], axis=0)
    alpha_ref[...] = whole[0:1, :] / whole[1:2, :]
    wait_part(sums.at[others], all_send, 2)


def solution(mesh):
    subs, cols = mesh.shape["sub"], mesh.shape["col"]
    count = subs * cols

    def step(rhs, schur, local_inverse, basis, coarse_inverse, primal_index, neighbour_dof):
        size, cases = rhs.shape[1:]
        face = size // 4
        primals = primal_index.shape[1]
        height, width = coarse_inverse.shape
        lanes = 128 * pl.cdiv(primals, 128)
        wide = 128 * pl.cdiv(width, 128)
        blocks = 5 * primals
        group = math.gcd(count, 32)
        anywhere = pl.BlockSpec(memory_space=pltpu.HBM)
        near = pl.BlockSpec(memory_space=pltpu.VMEM)
        fixed = 4 * size * size + 8 * face * face + 24 * size * cases + 8 * 128 * size
        slots = count * (4 * 8 * lanes + 2 * primals * cases * 2 + 4 * 8 * cases)
        coarse = 2 * subs * height * wide + 12 * cols * blocks * wide + 4 * count * primals * blocks
        limit = min(fixed + slots + coarse + 6 * 1024 * 1024, 63 * 1024 * 1024)
        first, alpha = pl.pallas_call(
            functools.partial(kernel, subs, cols),
            out_shape=(
                jax.ShapeDtypeStruct((size, cases), F32),
                jax.ShapeDtypeStruct((1, cases), F32),
            ),
            in_specs=[anywhere] * 7,
            out_specs=(near, near),
            scratch_shapes=[
                pltpu.VMEM(basis.shape, BF16),
                pltpu.VMEM(primal_index.shape, jnp.int32),
                pltpu.VMEM(neighbour_dof.shape, jnp.int32),
                pltpu.VMEM((size, cases), BF16),
                pltpu.VMEM((size, size), BF16),
                pltpu.VMEM((size, size), BF16),
                pltpu.VMEM((4, face, face), BF16),
                pltpu.VMEM((4, face, cases), BF16),
                pltpu.VMEM((4, face, cases), BF16),
                pltpu.VMEM((4, primals, face), BF16),
                pltpu.VMEM((4, face, 2 * primals), BF16),
                pltpu.VMEM((4, 2 * primals, cases), BF16),
                pltpu.VMEM((size, cases), F32),
                pltpu.VMEM((size, cases), BF16),
                pltpu.VMEM((size, cases), BF16),
                pltpu.VMEM((size, cases), F32),
                pltpu.VMEM((count, 1, lanes), F32),
                pltpu.VMEM((subs * height, width), BF16),
                pltpu.VMEM((cols * blocks, width), F32),
                pltpu.VMEM((cols, blocks, width), BF16),
                pltpu.VMEM((cols, blocks, width), BF16),
                pltpu.VMEM((count // group, blocks, group * primals), BF16),
                pltpu.VMEM((count, primals, cases), BF16),
                pltpu.VMEM((count, 2, cases), F32),
                pltpu.SemaphoreType.DMA((8,)),
                pltpu.SemaphoreType.DMA((4,)),
                pltpu.SemaphoreType.DMA((4,)),
                pltpu.SemaphoreType.DMA((4,)),
                pltpu.SemaphoreType.DMA((4,)),
                pltpu.SemaphoreType.DMA((4,)),
                pltpu.SemaphoreType.DMA((4,)),
                pltpu.SemaphoreType.DMA((5,)),
                pltpu.SemaphoreType.DMA((5,)),
                pltpu.SemaphoreType.REGULAR((4,)),
                pltpu.SemaphoreType.REGULAR((1,)),
            ],
            compiler_params=pltpu.CompilerParams(
                collective_id=0, has_side_effects=True, vmem_limit_bytes=limit
            ),
        )(*(pltpu.with_memory_space_constraint(x, pltpu.HBM) for x in (rhs, schur, local_inverse, basis, coarse_inverse, primal_index, neighbour_dof)))
        return (alpha * first).astype(BF16)[None]

    return jax.shard_map(
        step,
        mesh=mesh,
        in_specs=(
            P(("sub", "col"), None, None),
            P(("sub", "col"), None, None),
            P(("sub", "col"), None, None),
            P(("sub", "col"), None, None),
            P("sub", "col"),
            P(("sub", "col"), None),
            P(("sub", "col"), None),
        ),
        out_specs=P(("sub", "col"), None, None),
        check_vma=False,
    )
```

time: 29 us -> 27.5 us (0.948)
  Pallas kernels: 28.1 us -> 26.6 us
    pallas_call x1, Pallas kernels: 28.1 us -> 26.6 us  [step(): pl.pallas_call(functools.partial(kernel, subs, cols), out_shape=(jax.Shap...]
where the time goes in v1:
time: 27.5 us; the launch traced here: 27.3 us
  Pallas kernels  26.6 us (97%)
  other arithmetic  0.73 us (3%)
    pallas_call x1, Pallas kernels, step(): pl.pallas_call(functools.partial(kernel, subs, cols), out_shape=(jax.Shap...  26.6 us
    broadcast_in_dim x1, other arithmetic, step(): return (alpha * first).astype(BF16)[None]  0.73 us

profile of v1, /device:TPU:0, one launch (start us, length us, event | category | flops | bytes accessed | tf_op | source)
XLA Modules:
  0.0 27.3 jit_solution(11669808856338239352)
XLA Ops:
  0.0 26.6 %shard_map.73 = (f32[1024,128]{1,0:T(8,128)S(1)}, f32[1,128]{1,0:T(1,128)S(1)}) custom-call(bf16[1,1024,128]{2,1,0:T(8,128)(2,1)} %rhs_hbm.1, bf16[1,1024,1024]{2,1,0:T(8,128)(2,1)} %schur_hbm.1, bf16[1,1024,1024]{2,1,0:T(8,128)(2,1)} %inverse_hbm.1, bf16[1,8,1024]{2,1,0:T(8,128)(2,1)} %basis_hbm.1, bf16[32,64]{1,0:T(8,128)(2,1)} %coarse_hbm.1, ...), custom_call_target="tpu_custom_call" | custom-call | tf_op jit(solution)/shard_map/pallas_call | solution.py:380
  26.6 0.7 %fusion = bf16[1,1024,128]{2,1,0:T(8,128)(2,1)} fusion(f32[1024,128]{1,0:T(8,128)S(1)} %get-tuple-element.8, f32[128]{0:T(128)S(1)} %bitcast.3), kind=kLoop, calls=%fused_computation.1 | loop fusion | flops 262144 | bytes 786944 | tf_op jit(solution)/shard_map/broadcast_in_dim | solution.py:429

commit v2 on v1

--- a/solution.py
+++ b/solution.py
@@ -18,7 +18,7 @@
     rhs_hbm, schur_hbm, inverse_hbm, basis_hbm, coarse_hbm, index_hbm, links_hbm,
     first_ref, alpha_ref,
     basis_ref, index_ref, links_ref, rhs_ref, schur_ref, inverse_ref,
-    picks, halo_rhs, halo_z, halo_basis, lift, given, z_ref, z_half, p_half, image_ref,
+    picks, halo_rhs, halo_z, halo_basis, lift, lift_image, z_ref, z_half, image_ref,
     indices, slab, picked, chosen, arrived, columns, loads, sums,
     local_sem, halo_send, halo_recv, z_send, z_recv, basis_send, basis_recv, all_send, all_recv,
     face_ack, all_ack,
@@ -66,12 +66,12 @@
         lax.fori_loop(start, stop, body, 0)
 
     barrier = pltpu.get_barrier_semaphore()
-    loop(
-        me + 1, count,
-        lambda target: pl.semaphore_signal(
-            barrier, inc=1, device_id=place(target), device_id_type=MESH
-        ),
-    )
+
+    def signal(semaphore, target):
+        pl.semaphore_signal(semaphore, inc=1, device_id=target, device_id_type=MESH)
+
+    loop(0, subs - 1 - row, lambda q: signal(barrier, (subs - 1 - q, column)))
+    loop(column + 1, cols, lambda k: signal(barrier, (row, k)))
 
     small_loads = [
         pltpu.make_async_copy(source, target, local_sem.at[4 + number])
@@ -125,23 +125,17 @@
 
     @pl.when(me > 0)
     def _():
-        pl.semaphore_wait(barrier, me)
+        pl.semaphore_wait(barrier, row + column)
 
     for g in (1, 0, 2, 3):
         @pl.when(lower[g])
         def _(g=g):
-            pl.semaphore_signal(
-                face_ack.at[facing(g)], inc=1, device_id=partner(g), device_id_type=MESH
-            )
+            signal(face_ack.at[facing(g)], partner(g))
             rhs_copies[g].start()
             basis_copies[g].start()
 
-    loop(
-        0, me,
-        lambda target: pl.semaphore_signal(
-            all_ack.at[0], inc=1, device_id=place(target), device_id_type=MESH
-        ),
-    )
+    loop(0, row, lambda target: signal(all_ack.at[0], (target, column)))
+    loop(0, column, lambda target: signal(all_ack.at[0], (row, target)))
 
     def send_coarse(target):
         pltpu.make_async_remote_copy(
@@ -169,7 +163,6 @@
     lanes = indices.shape[2]
     indices[me] = jnp.zeros((1, lanes), F32)
     indices[me, :, pl.ds(0, primals)] = index_ref[...].astype(F32)
-    loop(0, me, lambda target: send_slot(indices, 0)(place(target)))
 
     offsets = (face, 0, 3 * face, 2 * face)
     for f in range(4):
@@ -186,10 +179,13 @@
 
     @pl.when(me < count - 1)
     def _():
-        pl.semaphore_wait(all_ack.at[0], count - 1 - me)
-
-    loop(row + 1, subs, send_coarse)
-    loop(me + 1, count, lambda target: send_slot(indices, 0)(place(target)))
+        pl.semaphore_wait(all_ack.at[0], subs + cols - 2 - row - column)
+
+    for step in range(1, cols):
+        signal(all_ack.at[1], (row, (column + step) % cols))
+    loop(0, subs - 1 - row, lambda q: send_coarse(subs - 1 - q))
+    pl.semaphore_wait(all_ack.at[1], cols - 1)
+    each_other(send_slot(indices, 0))
 
     def wait_face(target, recv, f):
         pltpu.make_async_copy(target.at[f], target.at[f], recv.at[f]).wait()
@@ -284,10 +280,18 @@
         wait_face(halo_basis, basis_recv, f)
         mine = basis_ref[0, :, f * face : (f + 1) * face].astype(F32) * 0.5
         theirs = halo_basis[f].astype(F32) * 0.5
-        both = jnp.concatenate([jnp.zeros_like(theirs), theirs], axis=0).astype(BF16)
+        none = jnp.zeros_like(theirs)
+        both = jnp.concatenate([none] * (f + 1) + [theirs] + [none] * (3 - f), axis=0).astype(BF16)
         turned = lax.dot_general(picks[f], both, (((1,), (1,)), ((), ())), preferred_element_type=F32)
-        kept = jnp.concatenate([mine, jnp.zeros_like(mine)], axis=0).T
-        lift[f] = (turned + kept).astype(BF16)
+        kept = jnp.concatenate([mine] + [none] * 4, axis=0).T
+        lift[f * face : (f + 1) * face, :] = (turned + kept).astype(BF16)
+
+    load_schur.wait()
+    for h in range(4):
+        rows = pl.ds(h * face, face)
+        lift_image[rows, :] = jnp.dot(
+            schur_ref[rows, :], lift[...], preferred_element_type=F32
+        ).astype(BF16)
 
     wait_part(arrived.at[pl.ds(0, cols - 1)], all_recv, 3)
 
@@ -305,6 +309,20 @@
 
     lax.fori_loop(0, count // group, arrange, 0)
 
+    for number, f in enumerate((2, 3, 1 - last, last)):
+        block = span(f)
+        wait_face(halo_z, z_recv, f)
+        value = z_ref[block, :] + jnp.dot(picks[f], halo_z[f], preferred_element_type=F32)
+        first_ref[block, :] = value
+        part = value.astype(BF16)
+        for h in range(4):
+            rows = pl.ds(h * face, face)
+            image = jnp.dot(schur_ref[rows, block], part, preferred_element_type=F32)
+            if number == 0:
+                image_ref[rows, :] = image
+            else:
+                image_ref[rows, :] += image
+
     wait_part(loads.at[others], all_recv, 1)
 
     def solve(g, total):
@@ -312,38 +330,17 @@
         return total + jnp.dot(columns[g], part.astype(BF16), preferred_element_type=F32)
 
     taken = lax.fori_loop(0, count // group, solve, jnp.zeros((blocks, cases), F32))
-    taken = taken.astype(BF16).astype(F32)
-    for f in range(4):
-        given[f] = jnp.concatenate(
-            [taken[:primals], taken[(f + 1) * primals : (f + 2) * primals]], axis=0
-        ).astype(BF16)
-    ended = jnp.sum(load * taken[:primals], axis=0, keepdims=True)
+    taken = taken.astype(BF16)
+    ended = jnp.sum(load * taken[:primals].astype(F32), axis=0, keepdims=True)
     sums[me, pl.ds(0, 1), :] = begun + ended
 
-    load_schur.wait()
-    for number, f in enumerate((2, 3, 1 - last, last)):
-        block = span(f)
-        first = z_ref[block, :] + jnp.dot(lift[f], given[f], preferred_element_type=F32)
-        wait_face(halo_z, z_recv, f)
-        first = first + jnp.dot(picks[f], halo_z[f], preferred_element_type=F32)
-        first_ref[block, :] = first
-        part = first.astype(BF16)
-        if number == 0:
-            for h in range(4):
-                rows = span(h)
-                image_ref[rows, :] = jnp.dot(schur_ref[rows, block], part, preferred_element_type=F32)
-        elif number < 3:
-            for h in range(4):
-                rows = span(h)
-                image_ref[rows, :] += jnp.dot(schur_ref[rows, block], part, preferred_element_type=F32)
-        else:
-            total = jnp.zeros((1, cases), F32)
-            for h in range(4):
-                rows = span(h)
-                image = image_ref[rows, :] + jnp.dot(
-                    schur_ref[rows, block], part, preferred_element_type=F32
-                )
-                total += jnp.sum(first_ref[rows, :] * image, axis=0, keepdims=True)
+    total = jnp.zeros((1, cases), F32)
+    for h in range(4):
+        rows = pl.ds(h * face, face)
+        value = first_ref[rows, :] + jnp.dot(lift[rows, :], taken, preferred_element_type=F32)
+        image = image_ref[rows, :] + jnp.dot(lift_image[rows, :], taken, preferred_element_type=F32)
+        first_ref[rows, :] = value
+        total += jnp.sum(value * image, axis=0, keepdims=True)
     sums[me, pl.ds(1, 1), :] = total
     each_other(send_slot(sums, 2))
     for copy in rhs_copies + basis_copies + z_copies:
@@ -396,10 +393,9 @@
                 pltpu.VMEM((4, face, cases), BF16),
                 pltpu.VMEM((4, face, cases), BF16),
                 pltpu.VMEM((4, primals, face), BF16),
-                pltpu.VMEM((4, face, 2 * primals), BF16),
-                pltpu.VMEM((4, 2 * primals, cases), BF16),
+                pltpu.VMEM((size, blocks), BF16),
+                pltpu.VMEM((size, blocks), BF16),
                 pltpu.VMEM((size, cases), F32),
-                pltpu.VMEM((size, cases), BF16),
                 pltpu.VMEM((size, cases), BF16),
                 pltpu.VMEM((size, cases), F32),
                 pltpu.VMEM((count, 1, lanes), F32),
@@ -420,7 +416,7 @@
                 pltpu.SemaphoreType.DMA((5,)),
                 pltpu.SemaphoreType.DMA((5,)),
                 pltpu.SemaphoreType.REGULAR((4,)),
-                pltpu.SemaphoreType.REGULAR((1,)),
+                pltpu.SemaphoreType.REGULAR((2,)),
             ],
             compiler_params=pltpu.CompilerParams(
                 collective_id=0, has_side_effects=True, vmem_limit_bytes=limit

time: 27.5 us -> 25.3 us (0.920)
  Pallas kernels: 26.6 us -> 24.4 us
    pallas_call x1, Pallas kernels: 26.6 us -> 24.4 us  [step(): pl.pallas_call(functools.partial(kernel, subs, cols), out_shape=(jax.Shap...]
where the time goes in v2:
time: 25.3 us; the launch traced here: 25.2 us
  Pallas kernels  24.4 us (96%)
  other arithmetic  0.73 us (3%)
    pallas_call x1, Pallas kernels, step(): pl.pallas_call(functools.partial(kernel, subs, cols), out_shape=(jax.Shap...  24.4 us
    broadcast_in_dim x1, other arithmetic, step(): return (alpha * first).astype(BF16)[None]  0.73 us

profile of v2, /device:TPU:0, one launch (start us, length us, event | category | flops | bytes accessed | tf_op | source)
XLA Modules:
  0.0 25.2 jit_solution(5138262104195445350)
XLA Ops:
  0.0 24.4 %shard_map.73 = (f32[1024,128]{1,0:T(8,128)S(1)}, f32[1,128]{1,0:T(1,128)S(1)}) custom-call(bf16[1,1024,128]{2,1,0:T(8,128)(2,1)} %rhs_hbm.1, bf16[1,1024,1024]{2,1,0:T(8,128)(2,1)} %schur_hbm.1, bf16[1,1024,1024]{2,1,0:T(8,128)(2,1)} %inverse_hbm.1, bf16[1,8,1024]{2,1,0:T(8,128)(2,1)} %basis_hbm.1, bf16[32,64]{1,0:T(8,128)(2,1)} %coarse_hbm.1, ...), custom_call_target="tpu_custom_call" | custom-call | tf_op jit(solution)/shard_map/pallas_call | solution.py:377
  24.4 0.7 %fusion = bf16[1,1024,128]{2,1,0:T(8,128)(2,1)} fusion(f32[1024,128]{1,0:T(8,128)S(1)} %get-tuple-element.8, f32[128]{0:T(128)S(1)} %bitcast.3), kind=kLoop, calls=%fused_computation.1 | loop fusion | flops 262144 | bytes 786944 | tf_op jit(solution)/shard_map/broadcast_in_dim | solution.py:425

commit v3 on v2

--- a/solution.py
+++ b/solution.py
@@ -11,6 +11,7 @@
 MESH = pl.DeviceIdType.MESH
 F32 = jnp.float32
 BF16 = jnp.bfloat16
+PIECES = 4
 
 
 def kernel(
@@ -197,35 +198,41 @@
 
     last = (row + 1) // subs
     load_rhs.wait()
-    load = jnp.zeros((primals, cases), F32)
     load_inverse.wait()
-    for number, f in enumerate((2, 3, 1 - last, last)):
+
+    def settle(f):
         block = span(f)
         wait_face(halo_rhs, halo_recv, f)
         got = jnp.dot(picks[f], halo_rhs[f], preferred_element_type=F32)
         residual = rhs_ref[block, :].astype(F32) + got
         first_ref[block, :] = residual
         part = (residual * 0.5).astype(BF16)
-        load += jnp.dot(basis_ref[0, :, block], part, preferred_element_type=F32)
-        if number == 0:
-            for h in range(4):
-                rows = span(h)
-                z_ref[rows, :] = jnp.dot(inverse_ref[rows, block], part, preferred_element_type=F32)
-        elif number < 3:
-            for h in range(4):
-                rows = span(h)
-                z_ref[rows, :] += jnp.dot(inverse_ref[rows, block], part, preferred_element_type=F32)
-        else:
-            for turn, h in enumerate((last, 1 - last, 2, 3)):
-                rows = span(h)
-                value = z_ref[rows, :] + jnp.dot(inverse_ref[rows, block], part, preferred_element_type=F32)
-                value = value * 0.5
-                z_ref[rows, :] = value
-                z_half[rows, :] = value.astype(BF16)
-                (row_z_copy(h) if turn < 2 else z_copies[h]).start()
-                if turn == 0:
-                    loads[me] = load.astype(BF16)
-                    each_other(send_slot(loads, 1))
+        return part, jnp.dot(basis_ref[0, :, block], part, preferred_element_type=F32)
+
+    part, load = settle(2)
+    other, more = settle(3)
+    load += more
+    part = jnp.concatenate([part, other], axis=0)
+    for h in range(PIECES):
+        rows = pl.ds(h * (size // PIECES), size // PIECES)
+        z_ref[rows, :] = jnp.dot(inverse_ref[rows, 2 * face :], part, preferred_element_type=F32)
+    part, more = settle(1 - last)
+    load += more
+    for h in range(PIECES):
+        rows = pl.ds(h * (size // PIECES), size // PIECES)
+        z_ref[rows, :] += jnp.dot(inverse_ref[rows, span(1 - last)], part, preferred_element_type=F32)
+    part, more = settle(last)
+    load += more
+    for turn, h in enumerate((last, 1 - last, 2, 3)):
+        rows = span(h)
+        value = z_ref[rows, :] + jnp.dot(inverse_ref[rows, span(last)], part, preferred_element_type=F32)
+        value = value * 0.5
+        z_ref[rows, :] = value
+        z_half[rows, :] = value.astype(BF16)
+        (row_z_copy(h) if turn < 2 else z_copies[h]).start()
+        if turn == 0:
+            loads[me] = load.astype(BF16)
+            each_other(send_slot(loads, 1))
     begun = jnp.sum(first_ref[...] * z_ref[...], axis=0, keepdims=True)
 
     def spread(start, extent, number):
@@ -293,6 +300,27 @@
             schur_ref[rows, :], lift[...], preferred_element_type=F32
         ).astype(BF16)
 
+    def meet(faces, fresh):
+        parts = []
+        for f in faces:
+            block = span(f)
+            wait_face(halo_z, z_recv, f)
+            value = z_ref[block, :] + jnp.dot(picks[f], halo_z[f], preferred_element_type=F32)
+            first_ref[block, :] = value
+            parts.append(value.astype(BF16))
+        part = parts[0] if len(parts) == 1 else jnp.concatenate(parts, axis=0)
+        wide = pl.ds(pl.multiple_of(faces[0] * face, face), len(faces) * face)
+        for h in range(PIECES):
+            rows = pl.ds(h * (size // PIECES), size // PIECES)
+            image = jnp.dot(schur_ref[rows, wide], part, preferred_element_type=F32)
+            if fresh:
+                image_ref[rows, :] = image
+            else:
+                image_ref[rows, :] += image
+
+    meet((2, 3), True)
+    meet((1 - last,), False)
+
     wait_part(arrived.at[pl.ds(0, cols - 1)], all_recv, 3)
 
     def arrange(g, carry):
@@ -309,19 +337,7 @@
 
     lax.fori_loop(0, count // group, arrange, 0)
 
-    for number, f in enumerate((2, 3, 1 - last, last)):
-        block = span(f)
-        wait_face(halo_z, z_recv, f)
-        value = z_ref[block, :] + jnp.dot(picks[f], halo_z[f], preferred_element_type=F32)
-        first_ref[block, :] = value
-        part = value.astype(BF16)
-        for h in range(4):
-            rows = pl.ds(h * face, face)
-            image = jnp.dot(schur_ref[rows, block], part, preferred_element_type=F32)
-            if number == 0:
-                image_ref[rows, :] = image
-            else:
-                image_ref[rows, :] += image
+    meet((last,), False)
 
     wait_part(loads.at[others], all_recv, 1)
 

time: 25.3 us -> 23.8 us (0.941)
  Pallas kernels: 24.4 us -> 22.9 us
    pallas_call x1, Pallas kernels: 24.4 us -> 22.9 us  [step(): pl.pallas_call(functools.partial(kernel, subs, cols), out_shape=(jax.Shap...]
where the time goes in v3:
time: 23.8 us; the launch traced here: 23.6 us
  Pallas kernels  22.9 us (96%)
  other arithmetic  0.73 us (3%)
    pallas_call x1, Pallas kernels, step(): pl.pallas_call(functools.partial(kernel, subs, cols), out_shape=(jax.Shap...  22.9 us
    broadcast_in_dim x1, other arithmetic, step(): return (alpha * first).astype(BF16)[None]  0.73 us

profile of v3, /device:TPU:0, one launch (start us, length us, event | category | flops | bytes accessed | tf_op | source)
XLA Modules:
  0.0 23.6 jit_solution(8761465066081773036)
XLA Ops:
  0.0 22.9 %shard_map.73 = (f32[1024,128]{1,0:T(8,128)S(1)}, f32[1,128]{1,0:T(1,128)S(1)}) custom-call(bf16[1,1024,128]{2,1,0:T(8,128)(2,1)} %rhs_hbm.1, bf16[1,1024,1024]{2,1,0:T(8,128)(2,1)} %schur_hbm.1, bf16[1,1024,1024]{2,1,0:T(8,128)(2,1)} %inverse_hbm.1, bf16[1,8,1024]{2,1,0:T(8,128)(2,1)} %basis_hbm.1, bf16[32,64]{1,0:T(8,128)(2,1)} %coarse_hbm.1, ...), custom_call_target="tpu_custom_call" | custom-call | tf_op jit(solution)/shard_map/pallas_call | solution.py:393
  22.9 0.7 %fusion = bf16[1,1024,128]{2,1,0:T(8,128)(2,1)} fusion(f32[1024,128]{1,0:T(8,128)S(1)} %get-tuple-element.8, f32[128]{0:T(128)S(1)} %bitcast.3), kind=kLoop, calls=%fused_computation.1 | loop fusion | flops 262144 | bytes 786944 | tf_op jit(solution)/shard_map/broadcast_in_dim | solution.py:441
